TPU v7x, 32 devices: a whole 2x2x4 slice. The times are simulated.
32 devices in a mesh: rep: 8 (over z, y), fsdp: 2 (over x), ctx: 2 (over core).
Axes of the slice: x: 2, y: 2, z: 4, core: 2. Of those that a mesh axis runs over, the one named last changes fastest.
Arguments:
- tokens: bfloat16 [32, 1024, 1280], P(('rep', 'fsdp'), 'ctx'), may hold values from -6 to 6
- prefixes: int32 [32], P(('rep', 'fsdp')), may hold values from 102 to 512, as said below
- query_weight: bfloat16 [1280, 1280], P(('fsdp', 'ctx')), may hold values from -0.15625 to 0.15625
- key_weight: bfloat16 [1280, 1280], P(('fsdp', 'ctx')), may hold values from -0.15625 to 0.15625
- value_weight: bfloat16 [1280, 1280], P(('fsdp', 'ctx')), may hold values from -0.15625 to 0.15625
- output_weight: bfloat16 [1280, 1280], P(('fsdp', 'ctx')), may hold values from -2 to 2
- up_weight: bfloat16 [1280, 1280], P(('fsdp', 'ctx')), may hold values from -0.15625 to 0.15625
- up_bias: float32 [1280], replicated, may hold values from -3 to 3
- down_weight: bfloat16 [1280, 1280], P(('fsdp', 'ctx')), may hold values from -0.15625 to 0.15625
- down_bias: float32 [1280], replicated, may hold values from -3 to 3
- attn_gain: float32 [1280], replicated, may hold values from 0.5 to 1.5
- mlp_gain: float32 [1280], replicated, may hold values from 0.5 to 1.5
- query_scale: float32 [80], replicated, may hold values from -2.5 to 2.5
- cotangent: bfloat16 [32, 1024, 1280], P(('rep', 'fsdp'), 'ctx'), may hold values from -6 to 6
Outputs:
- mixed: bfloat16 [32, 1024, 1280], P(('rep', 'fsdp'), 'ctx')
- tokens_grad: bfloat16 [32, 1024, 1280], P(('rep', 'fsdp'), 'ctx')
- query_grad: float32 [1280, 1280], P(('fsdp', 'ctx'))
- key_grad: float32 [1280, 1280], P(('fsdp', 'ctx'))
- value_grad: float32 [1280, 1280], P(('fsdp', 'ctx'))
- output_grad: float32 [1280, 1280], P(('fsdp', 'ctx'))
- up_grad: float32 [1280, 1280], P(('fsdp', 'ctx'))
- upbias_grad: float32 [1280], replicated
- down_grad: float32 [1280, 1280], P(('fsdp', 'ctx'))
- downbias_grad: float32 [1280], replicated
- attngain_grad: float32 [1280], replicated
- mlpgain_grad: float32 [1280], replicated
- scale_grad: float32 [80], replicated
Inputs may be any that keep to these rules, and one draw needn't show every extreme that they name: `prefixes`: at least one sequence has 1024 // 10 and one has 1024 // 2.
All inputs are finite; a program needn't handle non-finite values.
Results may differ from a plain program's by a relative error of at most 0.02.
Values may be sent and summed in bfloat16 or wider, within the bound.
No kernel may reach another device: no remote copies, remote signals or barrier semaphores. Data moves between devices by JAX's collectives and lax.ppermute only.
A program may use at most 384 MiB of HBM per device.

v0:
```python
import jax
import jax.numpy as jnp
from jax import lax
from jax.sharding import PartitionSpec as P

HD = 80
epsilon = 1e-06
softplus_gain = 1.442695041
masked_value = -1e30


def norm_factor(values):
    return lax.rsqrt(jnp.mean(values * values, axis=-1, keepdims=True) + epsilon)


def norm_back(upstream, values, factor, gain_vec):
    scaled = upstream * gain_vec
    row_inner = jnp.mean(scaled * values, axis=-1, keepdims=True)
    return factor * scaled - values * factor**3 * row_inner


def allowed_mask(offset, local_rows, length, prefix):
    row_index = offset + jnp.arange(local_rows, dtype=jnp.int32)[:, None]
    col_index = jnp.arange(length, dtype=jnp.int32)[None, :]
    return (col_index <= row_index) | (col_index < prefix)


def masked_scores(queries, keys, allowed):
    scores = jnp.einsum("qhe,khe->hqk", queries, keys, preferred_element_type=jnp.float32)
    return jnp.where(allowed[None], scores, masked_value)


def shards(
    tokens,
    prefixes,
    query_weight,
    key_weight,
    value_weight,
    output_weight,
    up_weight,
    up_bias,
    down_weight,
    down_bias,
    attn_gain,
    mlp_gain,
    query_scale,
    cotangent,
):
    seq_count, local_rows, model_width = tokens.shape
    head_count = model_width // HD
    position_index = lax.axis_index("ctx")
    offset = position_index * local_rows
    full_query, full_key, full_value, full_output, full_up, full_down = (
        lax.all_gather(query_weight, ("fsdp", "ctx"), axis=0, tiled=True),
        lax.all_gather(key_weight, ("fsdp", "ctx"), axis=0, tiled=True),
        lax.all_gather(value_weight, ("fsdp", "ctx"), axis=0, tiled=True),
        lax.all_gather(output_weight, ("fsdp", "ctx"), axis=0, tiled=True),
        lax.all_gather(up_weight, ("fsdp", "ctx"), axis=0, tiled=True),
        lax.all_gather(down_weight, ("fsdp", "ctx"), axis=0, tiled=True),
    )
    rows_in = tokens.reshape(seq_count * local_rows, model_width).astype(jnp.float32)
    factor_one = norm_factor(rows_in)
    normed = (rows_in * factor_one * attn_gain).astype(jnp.bfloat16)
    scale_soft = jax.nn.softplus(query_scale) * (softplus_gain * HD ** (-0.5))
    query_raw = jnp.dot(normed, full_query, preferred_element_type=jnp.float32).reshape(
        seq_count, local_rows, head_count, HD
    )
    queries = (query_raw * scale_soft).astype(jnp.bfloat16)
    key_local = (
        jnp.dot(normed, full_key, preferred_element_type=jnp.float32)
        .astype(jnp.bfloat16)
        .reshape(seq_count, local_rows, model_width)
    )
    value_local = (
        jnp.dot(normed, full_value, preferred_element_type=jnp.float32)
        .astype(jnp.bfloat16)
        .reshape(seq_count, local_rows, model_width)
    )
    key_all, value_all = (
        lax.all_gather(key_local, "ctx", axis=1, tiled=True),
        lax.all_gather(value_local, "ctx", axis=1, tiled=True),
    )
    length = key_all.shape[1]

    def forward_one(members):
        queries_seq, keys_seq, values_seq, prefix = members
        allowed = allowed_mask(offset, local_rows, length, prefix)
        scores = masked_scores(queries_seq, keys_seq.reshape(length, head_count, HD), allowed)
        row_max = jnp.max(scores, axis=-1, keepdims=True)
        weights = jnp.exp(scores - row_max)
        row_total = jnp.sum(weights, axis=-1, keepdims=True)
        probability = (weights / row_total).astype(jnp.bfloat16)
        context = jnp.einsum(
            "hqk,khe->qhe",
            probability,
            values_seq.reshape(length, head_count, HD),
            preferred_element_type=jnp.float32,
        )
        return (context, row_max + jnp.log(row_total))

    context, logsum = lax.map(forward_one, (queries, key_all, value_all, prefixes))
    attended = context.reshape(seq_count * local_rows, model_width).astype(jnp.bfloat16)
    middle = rows_in + jnp.dot(attended, full_output, preferred_element_type=jnp.float32)
    factor_two = norm_factor(middle)
    normed_two = (middle * factor_two * mlp_gain).astype(jnp.bfloat16)
    before = jnp.dot(normed_two, full_up, preferred_element_type=jnp.float32) + up_bias
    hidden = jax.nn.silu(before).astype(jnp.bfloat16)
    mixed_rows = middle + jnp.dot(hidden, full_down, preferred_element_type=jnp.float32) + down_bias
    mixed_out = mixed_rows.astype(jnp.bfloat16).reshape(seq_count, local_rows, model_width)
    key_back, value_back = (key_all, value_all)
    back_query, back_key, back_value, back_output, back_up, back_down = (
        lax.all_gather(query_weight, ("fsdp", "ctx"), axis=0, tiled=True),
        lax.all_gather(key_weight, ("fsdp", "ctx"), axis=0, tiled=True),
        lax.all_gather(value_weight, ("fsdp", "ctx"), axis=0, tiled=True),
        lax.all_gather(output_weight, ("fsdp", "ctx"), axis=0, tiled=True),
        lax.all_gather(up_weight, ("fsdp", "ctx"), axis=0, tiled=True),
        lax.all_gather(down_weight, ("fsdp", "ctx"), axis=0, tiled=True),
    )
    key_back, value_back = (
        lax.all_gather(key_local, "ctx", axis=1, tiled=True),
        lax.all_gather(value_local, "ctx", axis=1, tiled=True),
    )
    upstream = cotangent.reshape(seq_count * local_rows, model_width)
    upstream_wide = upstream.astype(jnp.float32)
    down_part = jnp.einsum("nf,nd->fd", hidden, upstream, preferred_element_type=jnp.float32)
    downbias_part = jnp.sum(upstream_wide, axis=0)
    hidden_grad = jnp.einsum("nd,fd->nf", upstream, back_down, preferred_element_type=jnp.float32)
    gate_sig = jax.nn.sigmoid(before)
    before_grad = (hidden_grad * gate_sig * (1.0 + before * (1.0 - gate_sig))).astype(jnp.bfloat16)
    up_part = jnp.einsum("nd,nf->df", normed_two, before_grad, preferred_element_type=jnp.float32)
    upbias_part = jnp.sum(before_grad.astype(jnp.float32), axis=0)
    normed_grad = jnp.einsum("nf,df->nd", before_grad, back_up, preferred_element_type=jnp.float32)
    mlpgain_part = jnp.sum(normed_grad * middle * factor_two, axis=0)
    middle_grad = upstream_wide + norm_back(normed_grad, middle, factor_two, mlp_gain)
    middle_low = middle_grad.astype(jnp.bfloat16)
    output_part = jnp.einsum("nd,ne->de", attended, middle_low, preferred_element_type=jnp.float32)
    context_grad = jnp.einsum(
        "ne,de->nd", middle_low, back_output, preferred_element_type=jnp.float32
    )
    context_grad = context_grad.astype(jnp.bfloat16).reshape(seq_count, local_rows, head_count, HD)

    def backward_one(members):
        queries_seq, keys_seq, values_seq, grad_seq, logsum_seq, prefix = members
        keys_heads = keys_seq.reshape(length, head_count, HD)
        values_heads = values_seq.reshape(length, head_count, HD)
        allowed = allowed_mask(offset, local_rows, length, prefix)
        scores = masked_scores(queries_seq, keys_heads, allowed)
        exact_prob = jnp.exp(scores - logsum_seq)
        probability = exact_prob.astype(jnp.bfloat16)
        prob_grad = jnp.einsum(
            "qhe,khe->hqk", grad_seq, values_heads, preferred_element_type=jnp.float32
        )
        row_inner = jnp.sum(prob_grad * exact_prob, axis=-1, keepdims=True)
        score_grad = (exact_prob * (prob_grad - row_inner)).astype(jnp.bfloat16)
        query_part = jnp.einsum(
            "hqk,khe->qhe", score_grad, keys_heads, preferred_element_type=jnp.float32
        )
        key_term = jnp.einsum(
            "hqk,qhe->khe", score_grad, queries_seq, preferred_element_type=jnp.float32
        )
        value_term = jnp.einsum(
            "hqk,qhe->khe", probability, grad_seq, preferred_element_type=jnp.float32
        )
        return (
            query_part,
            key_term.reshape(length, model_width),
            value_term.reshape(length, model_width),
        )

    query_seqgrad, key_partial, value_partial = lax.map(
        backward_one, (queries, key_back, value_back, context_grad, logsum, prefixes)
    )
    key_summed, value_summed = (
        lax.psum_scatter(key_partial, "ctx", scatter_dimension=1, tiled=True),
        lax.psum_scatter(value_partial, "ctx", scatter_dimension=1, tiled=True),
    )
    key_low = key_summed.astype(jnp.bfloat16).reshape(seq_count * local_rows, model_width)
    value_low = value_summed.astype(jnp.bfloat16).reshape(seq_count * local_rows, model_width)
    scaled_low = query_seqgrad.astype(jnp.bfloat16)
    query_low = (
        (scaled_low * scale_soft).astype(jnp.bfloat16).reshape(seq_count * local_rows, model_width)
    )
    scale_part = jnp.sum(scaled_low * query_raw, axis=(0, 1, 2))
    scale_part = scale_part * jax.nn.sigmoid(query_scale) * (softplus_gain * HD ** (-0.5))
    query_part = jnp.einsum("nd,ne->de", normed, query_low, preferred_element_type=jnp.float32)
    key_part = jnp.einsum("nd,ne->de", normed, key_low, preferred_element_type=jnp.float32)
    value_part = jnp.einsum("nd,ne->de", normed, value_low, preferred_element_type=jnp.float32)
    normed_grad_one = jnp.einsum(
        "ne,de->nd", query_low, back_query, preferred_element_type=jnp.float32
    )
    normed_grad_one = normed_grad_one + jnp.einsum(
        "ne,de->nd", key_low, back_key, preferred_element_type=jnp.float32
    )
    normed_grad_one = normed_grad_one + jnp.einsum(
        "ne,de->nd", value_low, back_value, preferred_element_type=jnp.float32
    )
    attngain_part = jnp.sum(normed_grad_one * rows_in * factor_one, axis=0)
    tokens_grad = middle_grad + norm_back(normed_grad_one, rows_in, factor_one, attn_gain)
    tokens_grad = tokens_grad.astype(jnp.bfloat16).reshape(seq_count, local_rows, model_width)
    query_shard, key_shard, value_shard, output_shard, up_shard, down_shard = (
        lax.psum_scatter(
            query_part.astype(jnp.bfloat16), ("fsdp", "ctx"), scatter_dimension=0, tiled=True
        ).astype(jnp.float32),
        lax.psum_scatter(
            key_part.astype(jnp.bfloat16), ("fsdp", "ctx"), scatter_dimension=0, tiled=True
        ).astype(jnp.float32),
        lax.psum_scatter(
            value_part.astype(jnp.bfloat16), ("fsdp", "ctx"), scatter_dimension=0, tiled=True
        ).astype(jnp.float32),
        lax.psum_scatter(
            output_part.astype(jnp.bfloat16), ("fsdp", "ctx"), scatter_dimension=0, tiled=True
        ).astype(jnp.float32),
        lax.psum_scatter(
            up_part.astype(jnp.bfloat16), ("fsdp", "ctx"), scatter_dimension=0, tiled=True
        ).astype(jnp.float32),
        lax.psum_scatter(
            down_part.astype(jnp.bfloat16), ("fsdp", "ctx"), scatter_dimension=0, tiled=True
        ).astype(jnp.float32),
    )
    query_total, key_total, value_total, output_total, up_total, down_total = (
        lax.psum(query_shard.astype(jnp.bfloat16), "rep").astype(jnp.float32),
        lax.psum(key_shard.astype(jnp.bfloat16), "rep").astype(jnp.float32),
        lax.psum(value_shard.astype(jnp.bfloat16), "rep").astype(jnp.float32),
        lax.psum(output_shard.astype(jnp.bfloat16), "rep").astype(jnp.float32),
        lax.psum(up_shard.astype(jnp.bfloat16), "rep").astype(jnp.float32),
        lax.psum(down_shard.astype(jnp.bfloat16), "rep").astype(jnp.float32),
    )
    upbias_total, downbias_total, attngain_total, mlpgain_total, scale_total = lax.psum(
        (upbias_part, downbias_part, attngain_part, mlpgain_part, scale_part),
        ("rep", "fsdp", "ctx"),
    )
    return (
        mixed_out,
        tokens_grad,
        query_total,
        key_total,
        value_total,
        output_total,
        up_total,
        upbias_total,
        down_total,
        downbias_total,
        attngain_total,
        mlpgain_total,
        scale_total,
    )


def solution(mesh):
    return jax.shard_map(
        shards,
        mesh=mesh,
        in_specs=(
            P(("rep", "fsdp"), "ctx", None),
            P(("rep", "fsdp")),
            P(("fsdp", "ctx"), None),
            P(("fsdp", "ctx"), None),
            P(("fsdp", "ctx"), None),
            P(("fsdp", "ctx"), None),
            P(("fsdp", "ctx"), None),
            P(),
            P(("fsdp", "ctx"), None),
            P(),
            P(),
            P(),
            P(),
            P(("rep", "fsdp"), "ctx", None),
        ),
        out_specs=(
            P(("rep", "fsdp"), "ctx", None),
            P(("rep", "fsdp"), "ctx", None),
            P(("fsdp", "ctx"), None),
            P(("fsdp", "ctx"), None),
            P(("fsdp", "ctx"), None),
            P(("fsdp", "ctx"), None),
            P(("fsdp", "ctx"), None),
            P(),
            P(("fsdp", "ctx"), None),
            P(),
            P(),
            P(),
            P(),
        ),
        check_vma=False,
    )
```

profile of v0, /device:TPU:0, one launch (start us, length us, event | category | flops | bytes accessed | tf_op | source)
XLA Modules:
  0.0 1070.1 jit_solution(11149948379400811405)
XLA Ops:
  15.3 26.3 %all-gather.15.cloned.1.call-done = bf16[1280,1280]{1,0:T(8,128)(2,1)} async-done(((bf16[320,1280]{1,0:T(8,128)(2,1)}), bf16[1280,1280]{1,0:T(8,128)(2,1)}) %all-gather.15.cloned.1.call-update) | async-done | bytes 3276816 | tf_op jit(solution)/shard_map/all_gather | solution.py:55
  53.9 18.5 %all-gather.9.cloned.1.call-done = bf16[1280,1280]{1,0:T(8,128)(2,1)} async-done(((bf16[320,1280]{1,0:T(8,128)(2,1)}), bf16[1280,1280]{1,0:T(8,128)(2,1)}) %all-gather.9.cloned.1.call-update) | async-done | bytes 3276816 | tf_op jit(solution)/shard_map/all_gather | solution.py:56
  119.9 18.4 %all-gather.11.cloned.1.call-done = bf16[2,1024,1280]{1,2,0:T(8,128)(2,1)} async-done(((bf16[2,512,1280]{1,2,0:T(8,128)(2,1)}), bf16[2,1024,1280]{1,2,0:T(8,128)(2,1)}) %all-gather.11.cloned.1.call-update) | async-done | bytes 5242896 | tf_op jit(solution)/shard_map/all_gather | solution.py:81
  140.1 103.8 %while.26 = (s32[]{:T(128)}, bf16[2,512,16,80]{1,3,2,0:T(8,128)(2,1)}, f32[2,16,512,1]{2,1,3,0:T(8,128)S(1)}, bf16[2,1024,1280]{1,2,0:T(8,128)(2,1)}, s32[]{:T(1...) while((s32[]{:T(128)}, ...), condition=%wide.region_4.5_spmd, body=%wide.region_1.4_spmd.sunk | while | flops 2760893952 | bytes 154147024 | solution.py:101
  159.9 15.4 %fusion.113 = f32[16,512]{1,0:T(8,128)S(1)} fusion(f32[16,512,1024]{2,1,0:T(8,128)} %get-tuple-element.332, f32[16,512]{1,0:T(8,128)S(1)} %get-tuple-element.333, pred[512,1024]{1,0:T(8,128)(4,1)S(1)} %fusion.112), kind=kLoop, calls=%fused_computation.3.clone.1 | loop fusion | flops 25157632 | bytes 34144256 | tf_op jit(solution)/shard_map/while/body/eval_jaxpr/reduce_sum | solution.py:91
  175.3 15.2 %bitcast_dynamic-update-slice_fusion.6 = bf16[2,512,16,80]{1,3,2,0:T(8,128)(2,1)S(1)} fusion(bf16[2,512,16,80]{1,3,2,0:T(8,128)(2,1)S(1)} %copy-done.8, s32[]{:T(128)S(6)} %copy.79, bf16[1024,16,80]{0,2,1:T(8,128)(2,1)S(1)} %bitcast.196, f32[16,512,1024]{2,1,0:T(8,128)} %get-tuple-element.332, f32[16,512]{1,0:T(8,128)S(1)} %fusion.113, ...), kind=kOutput, calls=%fused_computation.5.clone.1 | convolution fusion | flops 1375731712 | bytes 39387140 | tf_op jit(solution)/shard_map/while/body/eval_jaxpr/hqk,khe->qhe/dot_general | solution.py:93
  198.3 14.3 %select_reduce_fusion.2 = (f32[16,512]{1,0:T(8,128)S(1)}, f32[16,512,1024]{2,1,0:T(8,128)}) fusion(pred[512,1024]{1,0:T(8,128)(4,1)S(1)} %fusion.112, bf16[1024,16,80]{0,2,1:T(8,128)(2,1)S(1)} %bitcast.193, bf16[2,512,16,80]{1,3,2,0:T(8,128)(2,1)S(1)} %get-tuple-element.373, s32[]{:T(128)S(6)} %copy.79), kind=kOutput, calls=%fused_computation.2.clone.1 | convolution fusion | flops 1358946304 | bytes 38043652 | tf_op jit(solution)/shard_map/while/body/eval_jaxpr/qhe,khe->hqk/dot_general | solution.py:29
  212.6 15.3 %fusion.113 = f32[16,512]{1,0:T(8,128)S(1)} fusion(f32[16,512,1024]{2,1,0:T(8,128)} %get-tuple-element.332, f32[16,512]{1,0:T(8,128)S(1)} %get-tuple-element.333, pred[512,1024]{1,0:T(8,128)(4,1)S(1)} %fusion.112), kind=kLoop, calls=%fused_computation.3.clone.1 | loop fusion | flops 25157632 | bytes 34144256 | tf_op jit(solution)/shard_map/while/body/eval_jaxpr/reduce_sum | solution.py:91
  311.0 272.4 %while.27 = (s32[]{:T(128)}, bf16[2,512,16,80]{1,3,2,0:T(8,128)(2,1)}, f32[2,1024,1280]{2,1,0:T(8,128)}, f32[2,1024,1280]{2,1,0:T(8,128)}, bf16[2,1024,1280]{1,2...) while((s32[]{:T(128)}, ...), condition=%wide.region_9.10_spmd, body=%wide.region_7.9_spmd.sunk | while | flops 6812591616 | bytes 374577376 | solution.py:170
  317.9 14.5 %fusion.123 = f32[16,512,1024]{2,1,0:T(8,128)} fusion(bf16[1024,16,80]{0,2,1:T(8,128)(2,1)S(1)} %bitcast.190, bf16[2,512,16,80]{1,3,2,0:T(8,128)(2,1)} %copy-done, s32[]{:T(128)S(6)} %copy.89), kind=kOutput, calls=%fused_computation.34.clone.1 | convolution fusion | flops 1342177280 | bytes 37486596 | tf_op jit(solution)/shard_map/while/body/eval_jaxpr/qhe,khe->hqk/dot_general | solution.py:29
  332.4 17.1 %fusion.125 = f32[16,80,1024]{2,1,0:T(8,128)} fusion(f32[16,512,1024]{2,1,0:T(8,128)} %fusion.123, f32[16,512]{1,0:T(8,128)S(1)} %dynamic-slice_bitcast_fusion.2, pred[512,1024]{1,0:T(8,128)(4,1)S(1)} %fusion.124, bf16[2,512,16,80]{1,3,2,0:T(8,128)(2,1)} %get-tuple-element.409, s32[]{:T(128)S(6)} %copy.89), kind=kOutput, calls=%fused_computation.22.clone.1 | convolution fusion | flops 1367343104 | bytes 40665092 | tf_op jit(solution)/shard_map/while/body/eval_jaxpr/hqk,qhe->khe/dot_general | solution.py:161
  355.4 25.5 %multiply_reduce_fusion.5 = (f32[16,512]{1,0:T(8,128)S(1)}, f32[16,512,1024]{2,1,0:T(8,128)}) fusion(f32[16,512,1024]{2,1,0:T(8,128)} %fusion.123, f32[16,512]{1,0:T(8,128)S(1)} %dynamic-slice_bitcast_fusion.2, pred[512,1024]{1,0:T(8,128)(4,1)S(1)} %fusion.124, bf16[1024,16,80]{0,2,1:T(8,128)(2,1)} %bitcast.195, ...), kind=kOutput, calls=%fused_computation.19.clone.1 | convolution fusion | flops 1375723520 | bytes 71630848 | tf_op jit(solution)/shard_map/while/body/eval_jaxpr/qhe,khe->hqk/dot_general | solution.py:150
  380.9 27.8 %multiply_convert_fusion.10 = bf16[16,512,1024]{2,1,0:T(8,128)(2,1)} fusion(f32[16,512,1024]{2,1,0:T(8,128)} %get-tuple-element.345, f32[16,512,1024]{2,1,0:T(8,128)} %fusion.123, f32[16,512]{1,0:T(8,128)S(1)} %get-tuple-element.346, f32[16,512]{1,0:T(8,128)S(1)} %dynamic-slice_bitcast_fusion.2, pred[512,1024]{1,0:T(8,128)(4,1)S(1)} %fusion.124), kind=kLoop, calls=%fused_computation.18.clone.1 | loop fusion | flops 41943040 | bytes 84475904 | tf_op jit(solution)/shard_map/while/body/eval_jaxpr/convert_element_type | solution.py:154
  453.8 14.5 %fusion.123 = f32[16,512,1024]{2,1,0:T(8,128)} fusion(bf16[1024,16,80]{0,2,1:T(8,128)(2,1)S(1)} %bitcast.190, bf16[2,512,16,80]{1,3,2,0:T(8,128)(2,1)} %copy-done, s32[]{:T(128)S(6)} %copy.89), kind=kOutput, calls=%fused_computation.34.clone.1 | convolution fusion | flops 1342177280 | bytes 37486596 | tf_op jit(solution)/shard_map/while/body/eval_jaxpr/qhe,khe->hqk/dot_general | solution.py:29
  468.4 17.1 %fusion.125 = f32[16,80,1024]{2,1,0:T(8,128)} fusion(f32[16,512,1024]{2,1,0:T(8,128)} %fusion.123, f32[16,512]{1,0:T(8,128)S(1)} %dynamic-slice_bitcast_fusion.2, pred[512,1024]{1,0:T(8,128)(4,1)S(1)} %fusion.124, bf16[2,512,16,80]{1,3,2,0:T(8,128)(2,1)} %get-tuple-element.409, s32[]{:T(128)S(6)} %copy.89), kind=kOutput, calls=%fused_computation.22.clone.1 | convolution fusion | flops 1367343104 | bytes 40665092 | tf_op jit(solution)/shard_map/while/body/eval_jaxpr/hqk,qhe->khe/dot_general | solution.py:161
  491.3 25.5 %multiply_reduce_fusion.5 = (f32[16,512]{1,0:T(8,128)S(1)}, f32[16,512,1024]{2,1,0:T(8,128)}) fusion(f32[16,512,1024]{2,1,0:T(8,128)} %fusion.123, f32[16,512]{1,0:T(8,128)S(1)} %dynamic-slice_bitcast_fusion.2, pred[512,1024]{1,0:T(8,128)(4,1)S(1)} %fusion.124, bf16[1024,16,80]{0,2,1:T(8,128)(2,1)} %bitcast.195, ...), kind=kOutput, calls=%fused_computation.19.clone.1 | convolution fusion | flops 1375723520 | bytes 71630848 | tf_op jit(solution)/shard_map/while/body/eval_jaxpr/qhe,khe->hqk/dot_general | solution.py:150
  516.8 27.8 %multiply_convert_fusion.10 = bf16[16,512,1024]{2,1,0:T(8,128)(2,1)} fusion(f32[16,512,1024]{2,1,0:T(8,128)} %get-tuple-element.345, f32[16,512,1024]{2,1,0:T(8,128)} %fusion.123, f32[16,512]{1,0:T(8,128)S(1)} %get-tuple-element.346, f32[16,512]{1,0:T(8,128)S(1)} %dynamic-slice_bitcast_fusion.2, pred[512,1024]{1,0:T(8,128)(4,1)S(1)} %fusion.124), kind=kLoop, calls=%fused_computation.18.clone.1 | loop fusion | flops 41943040 | bytes 84475904 | tf_op jit(solution)/shard_map/while/body/eval_jaxpr/convert_element_type | solution.py:154
  667.0 41.2 %reduce-scatter.21.cloned.1.call-done = bf16[320,1280]{1,0:T(8,128)(2,1)} async-done(((bf16[1280,1280]{1,0:T(8,128)(2,1)}), bf16[320,1280]{1,0:T(8,128)(2,1)}) %reduce-scatter.21.cloned.1.call-update) | async-done | bytes 819216 | tf_op jit(solution)/shard_map/reduce_scatter | solution.py:213
  708.1 41.3 %reduce-scatter.19.cloned.1.call-done = bf16[320,1280]{1,0:T(8,128)(2,1)} async-done(((bf16[1280,1280]{1,0:T(8,128)(2,1)}), bf16[320,1280]{1,0:T(8,128)(2,1)}) %reduce-scatter.19.cloned.1.call-update) | async-done | bytes 819216 | tf_op jit(solution)/shard_map/reduce_scatter | solution.py:210
  749.4 41.2 %reduce-scatter.13.cloned.1.call-done = bf16[320,1280]{1,0:T(8,128)(2,1)} async-done(((bf16[1280,1280]{1,0:T(8,128)(2,1)}), bf16[320,1280]{1,0:T(8,128)(2,1)}) %reduce-scatter.13.cloned.1.call-update) | async-done | bytes 819216 | tf_op jit(solution)/shard_map/reduce_scatter | solution.py:201
  790.6 41.1 %reduce-scatter.17.cloned.1.call-done = bf16[320,1280]{1,0:T(8,128)(2,1)} async-done(((bf16[1280,1280]{1,0:T(8,128)(2,1)}), bf16[320,1280]{1,0:T(8,128)(2,1)}) %reduce-scatter.17.cloned.1.call-update) | async-done | bytes 819216 | tf_op jit(solution)/shard_map/reduce_scatter | solution.py:207
  831.7 41.2 %reduce-scatter.15.cloned.1.call-done = bf16[320,1280]{1,0:T(8,128)(2,1)} async-done(((bf16[1280,1280]{1,0:T(8,128)(2,1)}), bf16[320,1280]{1,0:T(8,128)(2,1)}) %reduce-scatter.15.cloned.1.call-update) | async-done | bytes 819216 | tf_op jit(solution)/shard_map/reduce_scatter | solution.py:204
  895.2 46.5 %all-reduce = (f32[1280]{0:T(1024)}, f32[1280]{0:T(1024)}, f32[1280]{0:T(1024)}, f32[1280]{0:T(1024)}, f32[80]{0:T(128)}) all-reduce(f32[1280]{0:T(1024)S(1)} %copy-done.33, f32[1280]{0:T(1024)S(1)} %convert_reduce_fusion, f32[1280]{0:T(1024)S(1)} %get-tuple-element.144, ...), channel_id=1, replica_groups=mesh['rep'=8,'fsdp'=2,'ctx'=2] {'rep','fsdp','ctx'}, use_global_device_ids=true, to_apply=%region_24.25 | all-reduce | flops 5200 | bytes 41600 | tf_op jit(solution)/shard_map/psum | solution.py:228
  947.7 105.4 %all-reduce.4.cloned.1.call-done = (bf16[320,1280]{1,0:T(8,128)(2,1)}, bf16[320,1280]{1,0:T(8,128)(2,1)}, bf16[320,1280]{1,0:T(8,128)(2,1)}, bf16[320,1280]{1,0:...) async-done(((bf16[320,1280]{1,0:T(8,128)(2,1)}, bf16[320,1280]{1,0:T(8,128)(2,1)}, bf16[320,1280]{1,0:T(8,128)(2,1)}, bf16[320,1280]{1,0:T(8,128)(2,1)}, ...) | async-done | bytes 4915216 | tf_op jit(solution)/shard_map/psum | solution.py:221
  (243 shorter events, 403.3 us)
Async XLA Ops:
  7.2 34.4 %all-gather.15.cloned.1.call-start = ((), (), s32[]{:S(2)}) async-start(), calls=%async_computation.11 | async-start | bytes 4096000 | tf_op jit(solution)/shard_map/all_gather | solution.py:55
  7.9 64.5 %all-gather.9.cloned.1.call-start = ((), (), s32[]{:S(2)}) async-start(), calls=%async_computation.8 | async-start | bytes 4096000 | tf_op jit(solution)/shard_map/all_gather | solution.py:56
  8.7 94.6 %all-gather.13.cloned.1.call-start = ((), (), s32[]{:S(2)}) async-start(), calls=%async_computation.10 | async-start | bytes 4096000 | tf_op jit(solution)/shard_map/all_gather | solution.py:54
  9.4 110.5 %all-gather.17.cloned.1.call-start = ((), (), s32[]{:S(2)}) async-start(), calls=%async_computation.12 | async-start | bytes 7864320 | tf_op jit(solution)/shard_map/all_gather | solution.py:80
  53.9 84.4 %all-gather.11.cloned.1.call-start = ((), (), s32[]{:S(2)}) async-start(), calls=%async_computation.9 | async-start | bytes 7864320 | tf_op jit(solution)/shard_map/all_gather | solution.py:81
  84.7 165.9 %all-gather.19.cloned.1.call-start = ((), (), s32[]{:S(2)}) async-start(), calls=%async_computation.13 | async-start | bytes 4096000 | tf_op jit(solution)/shard_map/all_gather | solution.py:57
  85.3 175.0 %all-gather.21.cloned.1.call-start = ((), (), s32[]{:S(2)}) async-start(), calls=%async_computation.14 | async-start | bytes 4096000 | tf_op jit(solution)/shard_map/all_gather | solution.py:58
  86.1 183.7 %all-gather.23.cloned.1.call-start = ((), (), s32[]{:S(2)}) async-start(), calls=%async_computation.15 | async-start | bytes 4096000 | tf_op jit(solution)/shard_map/all_gather | solution.py:59
  86.8 543.3 %reduce-scatter.11.cloned.1.call-start = ((), (), s32[]{:S(2)}) async-start(), calls=%async_computation.17 | async-start | bytes 15728640 | tf_op jit(solution)/shard_map/reduce_scatter | solution.py:175
  87.1 21.8 %copy-start.35 = (f32[80]{0:T(128)}, f32[80]{0:T(128)S(1)}, u32[]{:S(2)}) copy-start(f32[80]{0:T(128)S(1)} %fusion.51) | copy-start | bytes 964
  108.9 31.2 %copy-start.43 = (s32[2]{0:T(128)S(1)}, s32[2]{0:T(128)}, u32[]{:S(2)}) copy-start(s32[2]{0:T(128)} %param.19) | copy-start | bytes 28
  159.9 15.4 %copy-start.5 = (bf16[1,1024,1280]{1,2,0:T(8,128)(2,1)S(1)}, bf16[1,1024,1280]{1,2,0:T(8,128)(2,1)}, u32[]{:S(2)}) copy-start(bf16[1,1024,1280]{1,2,0:T(8,128)(2,1)} %get-tuple-element.330) | copy-start | bytes 7864324 | tf_op jit(solution)/shard_map/while
  159.9 15.4 %copy-start.8 = (bf16[2,512,16,80]{1,3,2,0:T(8,128)(2,1)S(1)}, bf16[2,512,16,80]{1,3,2,0:T(8,128)(2,1)}, u32[]{:S(2)}) copy-start(bf16[2,512,16,80]{1,3,2,0:T(8,128)(2,1)} %get-tuple-element.359) | copy-start | bytes 7864324 | tf_op jit(solution)/shard_map/while
  212.6 15.4 %copy-start.8 = (bf16[2,512,16,80]{1,3,2,0:T(8,128)(2,1)S(1)}, bf16[2,512,16,80]{1,3,2,0:T(8,128)(2,1)}, u32[]{:S(2)}) copy-start(bf16[2,512,16,80]{1,3,2,0:T(8,128)(2,1)} %get-tuple-element.359) | copy-start | bytes 7864324 | tf_op jit(solution)/shard_map/while
  260.3 24.0 %copy-start.29 = (f32[1024]{0:T(1024)}, f32[1024]{0:T(1024)S(1)}, u32[]{:S(2)}) copy-start(f32[1024]{0:T(1024)S(1)} %get-tuple-element.206) | copy-start | bytes 12292
  583.4 56.1 %reduce-scatter.9.cloned.1.call-start = ((), (), s32[]{:S(2)}) async-start(), calls=%async_computation.16 | async-start | bytes 15728640 | tf_op jit(solution)/shard_map/reduce_scatter | solution.py:174
  584.0 82.9 %reduce-scatter.23.cloned.1.call-start = ((), (), s32[]{:S(2)}) async-start(), calls=%async_computation.23 | async-start | bytes 4096000 | tf_op jit(solution)/shard_map/reduce_scatter | solution.py:216
  594.3 113.9 %reduce-scatter.21.cloned.1.call-start = ((), (), s32[]{:S(2)}) async-start(), calls=%async_computation.22 | async-start | bytes 4096000 | tf_op jit(solution)/shard_map/reduce_scatter | solution.py:213
  605.8 143.6 %reduce-scatter.19.cloned.1.call-start = ((), (), s32[]{:S(2)}) async-start(), calls=%async_computation.21 | async-start | bytes 4096000 | tf_op jit(solution)/shard_map/reduce_scatter | solution.py:210
  613.3 177.3 %reduce-scatter.13.cloned.1.call-start = ((), (), s32[]{:S(2)}) async-start(), calls=%async_computation.18 | async-start | bytes 4096000 | tf_op jit(solution)/shard_map/reduce_scatter | solution.py:201
  630.0 201.7 %reduce-scatter.17.cloned.1.call-start = ((), (), s32[]{:S(2)}) async-start(), calls=%async_computation.20 | async-start | bytes 4096000 | tf_op jit(solution)/shard_map/reduce_scatter | solution.py:207
  639.4 233.5 %reduce-scatter.15.cloned.1.call-start = ((), (), s32[]{:S(2)}) async-start(), calls=%async_computation.19 | async-start | bytes 4096000 | tf_op jit(solution)/shard_map/reduce_scatter | solution.py:204
  651.4 401.7 %all-reduce.4.cloned.1.call-start = ((), (), s32[]{:S(2)}) async-start(), calls=%async_computation.24 | async-start | bytes 9830400 | tf_op jit(solution)/shard_map/psum | solution.py:221
  652.2 220.7 %copy-start.40 = (f32[1280]{0:T(1024)S(1)}, f32[1280]{0:T(1024)}, u32[]{:S(2)}) copy-start(f32[1280]{0:T(1024)} %param.27) | copy-start | bytes 15364
  (47 other events, 285.5 us)
Sparse Core Ops, SparseCore 0:
  9.6 31.9 all-gather.14
  43.1 29.2 all-gather.8
  74.0 29.2 all-gather.12
  104.7 15.2 all-gather.16
  121.9 16.3 all-gather.10
  139.7 30.4 all-gather.18
  171.7 29.2 all-gather.20
  202.6 29.2 all-gather.22
  583.5 19.3 reduce-scatter.10
  605.0 19.2 reduce-scatter.8
  626.9 39.9 reduce-scatter.22
  669.4 38.6 reduce-scatter.20
  710.7 38.6 reduce-scatter.18
  751.8 38.6 reduce-scatter.12
  793.0 38.6 reduce-scatter.16
  834.1 38.6 reduce-scatter.14
  877.1 175.9 all-reduce.3
where the time goes:
time: 1080 us; the launch traced here: 1070 us
  waiting for transfers between devices  401 us (37%)
  matrix products  357 us (33%)
  other arithmetic  131 us (12%)
  local copies, waits for them, and re-layouts  118 us (11%)
  blocking collectives  46.5 us (4%)
  between operations  14.7 us (1%)
    psum x1, waiting for transfers between devices, shards(): lax.psum(query_shard.astype(jnp.bfloat16), 'rep').astype(jnp.float32)  105 us
    dot_general x4, matrix products, masked_scores(): jnp.einsum('qhe,khe->hqk', queries, keys, preferred_element_type=jnp.floa...  57 us
    convert_element_type x2, other arithmetic, backward_one(): score_grad = (exact_prob * (prob_grad - row_inner)).astype(jnp.bfloat16)  55.7 us
    dot_general x2, matrix products, backward_one(): jnp.einsum('qhe,khe->hqk', grad_seq, values_heads, preferred_element_type...  51 us
    psum x1, blocking collectives, shards(): lax.psum((upbias_part, downbias_part, attngain_part, mlpgain_part, scale_...  46.5 us
    reduce_scatter x1, waiting for transfers between devices, shards(): lax.psum_scatter(output_part.astype(jnp.bfloat16), ('fsdp', 'ctx'), scatt...  41.3 us
    dynamic_update_slice x6, local copies, waits for them, and re-layouts, shards(): lax.map(backward_one, (queries, key_back, value_back, context_grad, logsu...  41.2 us
    reduce_scatter x1, waiting for transfers between devices, shards(): lax.psum_scatter(up_part.astype(jnp.bfloat16), ('fsdp', 'ctx'), scatter_d...  41.2 us
  transfers between devices with their start and end apart: 17, of which 12 were waited for; matrix products, arithmetic and copies ran while one was open for 25% of the time, Pallas kernels for 0%

commit v1 on v0

--- a/solution.py
+++ b/solution.py
@@ -7,6 +7,18 @@
 epsilon = 1e-06
 softplus_gain = 1.442695041
 masked_value = -1e30
+
+
+def gather_by_bits(array, axis, dim):
+    ways, here, step = (lax.axis_size(axis), lax.axis_index(axis), array.shape[dim])
+    line, have = (array, 1)
+    while have < ways:
+        line = jnp.concatenate(
+            [line, lax.ppermute(line, axis, [(d, (d - have) % ways) for d in range(ways)])],
+            axis=dim,
+        )
+        have = 2 * have
+    return jnp.roll(line, here * step, axis=dim)
 
 
 def norm_factor(values):
@@ -52,7 +64,7 @@
     offset = position_index * local_rows
     full_query, full_key, full_value, full_output, full_up, full_down = (
         lax.all_gather(query_weight, ("fsdp", "ctx"), axis=0, tiled=True),
-        lax.all_gather(key_weight, ("fsdp", "ctx"), axis=0, tiled=True),
+        gather_by_bits(key_weight, ("fsdp", "ctx"), 0),
         lax.all_gather(value_weight, ("fsdp", "ctx"), axis=0, tiled=True),
         lax.all_gather(output_weight, ("fsdp", "ctx"), axis=0, tiled=True),
         lax.all_gather(up_weight, ("fsdp", "ctx"), axis=0, tiled=True),

time: 1080 us -> 1100 us (1.019)
  waiting for transfers between devices: 401 us -> 425 us
    ppermute x0 -> x2, waiting for transfers between devices: none -> 67.9 us  [gather_by_bits(): lax.ppermute(line, axis, [(d, (d - have) % ways) for d in range(ways)])]
    all_gather x1, waiting for transfers between devices: 18.5 us -> 0.02 us  [shards(): lax.all_gather(value_weight, ('fsdp', 'ctx'), axis=0, tiled=True)]
    all_gather x1, waiting for transfers between devices: 14 us -> 0.01 us  [shards(): lax.all_gather(query_weight, ('fsdp', 'ctx'), axis=0, tiled=True)]
    all_gather x1, waiting for transfers between devices: 18.4 us -> 4.71 us  [shards(): lax.all_gather(value_local, 'ctx', axis=1, tiled=True)]
  transfers between devices with their start and end apart: 17 -> 19, of which waited for: 12 -> 11; matrix products, arithmetic and copies ran while one was open for 25% -> 25% of each run, Pallas kernels for 0% -> 0%
where the time goes in v1:
time: 1100 us
  waiting for transfers between devices  425 us (39%)
  matrix products  354 us (32%)
  other arithmetic  129 us (12%)
  local copies, waits for them, and re-layouts  123 us (11%)
  blocking collectives  46.6 us (4%)
  between operations  14.8 us (1%)
    psum x1, waiting for transfers between devices, shards(): lax.psum(query_shard.astype(jnp.bfloat16), 'rep').astype(jnp.float32)  115 us
    ppermute x2, waiting for transfers between devices, gather_by_bits(): lax.ppermute(line, axis, [(d, (d - have) % ways) for d in range(ways)])  67.9 us
    dot_general x4, matrix products, masked_scores(): jnp.einsum('qhe,khe->hqk', queries, keys, preferred_element_type=jnp.floa...  56.9 us
    convert_element_type x2, other arithmetic, backward_one(): score_grad = (exact_prob * (prob_grad - row_inner)).astype(jnp.bfloat16)  55.7 us
    dot_general x2, matrix products, backward_one(): jnp.einsum('qhe,khe->hqk', grad_seq, values_heads, preferred_element_type...  50.8 us
    psum x1, blocking collectives, shards(): lax.psum((upbias_part, downbias_part, attngain_part, mlpgain_part, scale_...  46.6 us
    reduce_scatter x1, waiting for transfers between devices, shards(): lax.psum_scatter(up_part.astype(jnp.bfloat16), ('fsdp', 'ctx'), scatter_d...  41.3 us
    reduce_scatter x1, waiting for transfers between devices, shards(): lax.psum_scatter(query_part.astype(jnp.bfloat16), ('fsdp', 'ctx'), scatte...  41.3 us
  transfers between devices with their start and end apart: 19, of which 11 were waited for; matrix products, arithmetic and copies ran while one was open for 25% of the time, Pallas kernels for 0%

profile of v1, /device:TPU:0, one launch (start us, length us, event | category | flops | bytes accessed | tf_op | source)
XLA Modules:
  0.0 1097.3 jit_solution(15169955081369782000)
XLA Ops:
  29.1 55.9 %collective-permute-done.1 = bf16[640,1280]{1,0:T(8,128)(2,1)} collective-permute-done((bf16[640,1280]{1,0:T(8,128)(2,1)}, bf16[640,1280]{1,0:T(8,128)(2,1)}, u32[]{:S(2)}, u32[]{:S(2)}) %collective-permute-start.1) | collective-permute-done | bytes 1638432 | tf_op jit(solution)/shard_map/ppermute | solution.py:17
  136.6 103.9 %while.26 = (s32[]{:T(128)}, bf16[2,512,16,80]{1,3,2,0:T(8,128)(2,1)}, f32[2,16,512,1]{2,1,3,0:T(8,128)S(1)}, bf16[2,1024,1280]{1,2,0:T(8,128)(2,1)}, s32[]{:T(1...) while((s32[]{:T(128)}, ...), condition=%wide.region_4.5_spmd, body=%wide.region_1.4_spmd.sunk | while | flops 2760893952 | bytes 154147024 | solution.py:113
  156.4 15.4 %fusion.114 = f32[16,512]{1,0:T(8,128)S(1)} fusion(f32[16,512,1024]{2,1,0:T(8,128)} %get-tuple-element.332, f32[16,512]{1,0:T(8,128)S(1)} %get-tuple-element.333, pred[512,1024]{1,0:T(8,128)(4,1)S(1)} %fusion.113), kind=kLoop, calls=%fused_computation.3.clone.1 | loop fusion | flops 25157632 | bytes 34144256 | tf_op jit(solution)/shard_map/while/body/eval_jaxpr/reduce_sum | solution.py:103
  171.8 15.2 %bitcast_dynamic-update-slice_fusion.6 = bf16[2,512,16,80]{1,3,2,0:T(8,128)(2,1)S(1)} fusion(bf16[2,512,16,80]{1,3,2,0:T(8,128)(2,1)S(1)} %copy-done.9, s32[]{:T(128)S(6)} %copy.84, bf16[1024,16,80]{0,2,1:T(8,128)(2,1)S(1)} %bitcast.195, f32[16,512,1024]{2,1,0:T(8,128)} %get-tuple-element.332, f32[16,512]{1,0:T(8,128)S(1)} %fusion.114, ...), kind=kOutput, calls=%fused_computation.5.clone.1 | convolution fusion | flops 1375731712 | bytes 39387140 | tf_op jit(solution)/shard_map/while/body/eval_jaxpr/hqk,khe->qhe/dot_general | solution.py:105
  194.8 14.3 %select_reduce_fusion.2 = (f32[16,512]{1,0:T(8,128)S(1)}, f32[16,512,1024]{2,1,0:T(8,128)}) fusion(pred[512,1024]{1,0:T(8,128)(4,1)S(1)} %fusion.113, bf16[1024,16,80]{0,2,1:T(8,128)(2,1)S(1)} %bitcast.192, bf16[2,512,16,80]{1,3,2,0:T(8,128)(2,1)S(1)} %get-tuple-element.373, s32[]{:T(128)S(6)} %copy.84), kind=kOutput, calls=%fused_computation.2.clone.1 | convolution fusion | flops 1358946304 | bytes 38043652 | tf_op jit(solution)/shard_map/while/body/eval_jaxpr/qhe,khe->hqk/dot_general | solution.py:41
  209.2 15.3 %fusion.114 = f32[16,512]{1,0:T(8,128)S(1)} fusion(f32[16,512,1024]{2,1,0:T(8,128)} %get-tuple-element.332, f32[16,512]{1,0:T(8,128)S(1)} %get-tuple-element.333, pred[512,1024]{1,0:T(8,128)(4,1)S(1)} %fusion.113), kind=kLoop, calls=%fused_computation.3.clone.1 | loop fusion | flops 25157632 | bytes 34144256 | tf_op jit(solution)/shard_map/while/body/eval_jaxpr/reduce_sum | solution.py:103
  224.6 14.3 %bitcast_dynamic-update-slice_fusion.6 = bf16[2,512,16,80]{1,3,2,0:T(8,128)(2,1)S(1)} fusion(bf16[2,512,16,80]{1,3,2,0:T(8,128)(2,1)S(1)} %copy-done.9, s32[]{:T(128)S(6)} %copy.84, bf16[1024,16,80]{0,2,1:T(8,128)(2,1)S(1)} %bitcast.195, f32[16,512,1024]{2,1,0:T(8,128)} %get-tuple-element.332, f32[16,512]{1,0:T(8,128)S(1)} %fusion.114, ...), kind=kOutput, calls=%fused_computation.5.clone.1 | convolution fusion | flops 1375731712 | bytes 39387140 | tf_op jit(solution)/shard_map/while/body/eval_jaxpr/hqk,khe->qhe/dot_general | solution.py:105
  307.5 272.2 %while.27 = (s32[]{:T(128)}, bf16[2,512,16,80]{1,3,2,0:T(8,128)(2,1)}, f32[2,1024,1280]{2,1,0:T(8,128)}, f32[2,1024,1280]{2,1,0:T(8,128)}, bf16[2,1024,1280]{1,2...) while((s32[]{:T(128)}, ...), condition=%wide.region_9.10_spmd, body=%wide.region_7.9_spmd.sunk | while | flops 6812591616 | bytes 374577376 | solution.py:182
  314.4 14.5 %fusion.124 = f32[16,512,1024]{2,1,0:T(8,128)} fusion(bf16[1024,16,80]{0,2,1:T(8,128)(2,1)S(1)} %bitcast.189, bf16[2,512,16,80]{1,3,2,0:T(8,128)(2,1)} %copy-done, s32[]{:T(128)S(6)} %copy.94), kind=kOutput, calls=%fused_computation.34.clone.1 | convolution fusion | flops 1342177280 | bytes 37486596 | tf_op jit(solution)/shard_map/while/body/eval_jaxpr/qhe,khe->hqk/dot_general | solution.py:41
  328.9 17.1 %fusion.126 = f32[16,80,1024]{2,1,0:T(8,128)} fusion(f32[16,512,1024]{2,1,0:T(8,128)} %fusion.124, f32[16,512]{1,0:T(8,128)S(1)} %dynamic-slice_bitcast_fusion.2, pred[512,1024]{1,0:T(8,128)(4,1)S(1)} %fusion.125, bf16[2,512,16,80]{1,3,2,0:T(8,128)(2,1)} %get-tuple-element.409, s32[]{:T(128)S(6)} %copy.94), kind=kOutput, calls=%fused_computation.22.clone.1 | convolution fusion | flops 1367343104 | bytes 40665092 | tf_op jit(solution)/shard_map/while/body/eval_jaxpr/hqk,qhe->khe/dot_general | solution.py:173
  351.9 25.4 %multiply_reduce_fusion.5 = (f32[16,512]{1,0:T(8,128)S(1)}, f32[16,512,1024]{2,1,0:T(8,128)}) fusion(f32[16,512,1024]{2,1,0:T(8,128)} %fusion.124, f32[16,512]{1,0:T(8,128)S(1)} %dynamic-slice_bitcast_fusion.2, pred[512,1024]{1,0:T(8,128)(4,1)S(1)} %fusion.125, bf16[1024,16,80]{0,2,1:T(8,128)(2,1)} %bitcast.194, ...), kind=kOutput, calls=%fused_computation.19.clone.1 | convolution fusion | flops 1375723520 | bytes 71630848 | tf_op jit(solution)/shard_map/while/body/eval_jaxpr/qhe,khe->hqk/dot_general | solution.py:162
  377.3 27.9 %multiply_convert_fusion.10 = bf16[16,512,1024]{2,1,0:T(8,128)(2,1)} fusion(f32[16,512,1024]{2,1,0:T(8,128)} %get-tuple-element.345, f32[16,512,1024]{2,1,0:T(8,128)} %fusion.124, f32[16,512]{1,0:T(8,128)S(1)} %get-tuple-element.346, f32[16,512]{1,0:T(8,128)S(1)} %dynamic-slice_bitcast_fusion.2, pred[512,1024]{1,0:T(8,128)(4,1)S(1)} %fusion.125), kind=kLoop, calls=%fused_computation.18.clone.1 | loop fusion | flops 41943040 | bytes 84475904 | tf_op jit(solution)/shard_map/while/body/eval_jaxpr/convert_element_type | solution.py:166
  450.2 14.5 %fusion.124 = f32[16,512,1024]{2,1,0:T(8,128)} fusion(bf16[1024,16,80]{0,2,1:T(8,128)(2,1)S(1)} %bitcast.189, bf16[2,512,16,80]{1,3,2,0:T(8,128)(2,1)} %copy-done, s32[]{:T(128)S(6)} %copy.94), kind=kOutput, calls=%fused_computation.34.clone.1 | convolution fusion | flops 1342177280 | bytes 37486596 | tf_op jit(solution)/shard_map/while/body/eval_jaxpr/qhe,khe->hqk/dot_general | solution.py:41
  464.7 17.1 %fusion.126 = f32[16,80,1024]{2,1,0:T(8,128)} fusion(f32[16,512,1024]{2,1,0:T(8,128)} %fusion.124, f32[16,512]{1,0:T(8,128)S(1)} %dynamic-slice_bitcast_fusion.2, pred[512,1024]{1,0:T(8,128)(4,1)S(1)} %fusion.125, bf16[2,512,16,80]{1,3,2,0:T(8,128)(2,1)} %get-tuple-element.409, s32[]{:T(128)S(6)} %copy.94), kind=kOutput, calls=%fused_computation.22.clone.1 | convolution fusion | flops 1367343104 | bytes 40665092 | tf_op jit(solution)/shard_map/while/body/eval_jaxpr/hqk,qhe->khe/dot_general | solution.py:173
  487.7 25.4 %multiply_reduce_fusion.5 = (f32[16,512]{1,0:T(8,128)S(1)}, f32[16,512,1024]{2,1,0:T(8,128)}) fusion(f32[16,512,1024]{2,1,0:T(8,128)} %fusion.124, f32[16,512]{1,0:T(8,128)S(1)} %dynamic-slice_bitcast_fusion.2, pred[512,1024]{1,0:T(8,128)(4,1)S(1)} %fusion.125, bf16[1024,16,80]{0,2,1:T(8,128)(2,1)} %bitcast.194, ...), kind=kOutput, calls=%fused_computation.19.clone.1 | convolution fusion | flops 1375723520 | bytes 71630848 | tf_op jit(solution)/shard_map/while/body/eval_jaxpr/qhe,khe->hqk/dot_general | solution.py:162
  513.1 27.9 %multiply_convert_fusion.10 = bf16[16,512,1024]{2,1,0:T(8,128)(2,1)} fusion(f32[16,512,1024]{2,1,0:T(8,128)} %get-tuple-element.345, f32[16,512,1024]{2,1,0:T(8,128)} %fusion.124, f32[16,512]{1,0:T(8,128)S(1)} %get-tuple-element.346, f32[16,512]{1,0:T(8,128)S(1)} %dynamic-slice_bitcast_fusion.2, pred[512,1024]{1,0:T(8,128)(4,1)S(1)} %fusion.125), kind=kLoop, calls=%fused_computation.18.clone.1 | loop fusion | flops 41943040 | bytes 84475904 | tf_op jit(solution)/shard_map/while/body/eval_jaxpr/convert_element_type | solution.py:166
  663.2 41.3 %reduce-scatter.21.cloned.1.call-done = bf16[320,1280]{1,0:T(8,128)(2,1)} async-done(((bf16[1280,1280]{1,0:T(8,128)(2,1)}), bf16[320,1280]{1,0:T(8,128)(2,1)}) %reduce-scatter.21.cloned.1.call-update) | async-done | bytes 819216 | tf_op jit(solution)/shard_map/reduce_scatter | solution.py:225
  704.5 41.2 %reduce-scatter.19.cloned.1.call-done = bf16[320,1280]{1,0:T(8,128)(2,1)} async-done(((bf16[1280,1280]{1,0:T(8,128)(2,1)}), bf16[320,1280]{1,0:T(8,128)(2,1)}) %reduce-scatter.19.cloned.1.call-update) | async-done | bytes 819216 | tf_op jit(solution)/shard_map/reduce_scatter | solution.py:222
  745.7 41.3 %reduce-scatter.13.cloned.1.call-done = bf16[320,1280]{1,0:T(8,128)(2,1)} async-done(((bf16[1280,1280]{1,0:T(8,128)(2,1)}), bf16[320,1280]{1,0:T(8,128)(2,1)}) %reduce-scatter.13.cloned.1.call-update) | async-done | bytes 819216 | tf_op jit(solution)/shard_map/reduce_scatter | solution.py:213
  787.0 41.2 %reduce-scatter.17.cloned.1.call-done = bf16[320,1280]{1,0:T(8,128)(2,1)} async-done(((bf16[1280,1280]{1,0:T(8,128)(2,1)}), bf16[320,1280]{1,0:T(8,128)(2,1)}) %reduce-scatter.17.cloned.1.call-update) | async-done | bytes 819216 | tf_op jit(solution)/shard_map/reduce_scatter | solution.py:219
  828.2 41.1 %reduce-scatter.15.cloned.1.call-done = bf16[320,1280]{1,0:T(8,128)(2,1)} async-done(((bf16[1280,1280]{1,0:T(8,128)(2,1)}), bf16[320,1280]{1,0:T(8,128)(2,1)}) %reduce-scatter.15.cloned.1.call-update) | async-done | bytes 819216 | tf_op jit(solution)/shard_map/reduce_scatter | solution.py:216
  880.1 19.9 %all-gather.23.cloned.1.call-done = bf16[1280,1280]{1,0:T(8,128)(2,1)} async-done(((bf16[320,1280]{1,0:T(8,128)(2,1)}), bf16[1280,1280]{1,0:T(8,128)(2,1)}) %all-gather.23.cloned.1.call-update) | async-done | bytes 3276816 | tf_op jit(solution)/shard_map/all_gather | solution.py:125
  913.1 46.6 %all-reduce = (f32[1280]{0:T(1024)}, f32[1280]{0:T(1024)}, f32[1280]{0:T(1024)}, f32[1280]{0:T(1024)}, f32[80]{0:T(128)}) all-reduce(f32[1280]{0:T(1024)S(1)} %copy-done.34, f32[1280]{0:T(1024)S(1)} %convert_reduce_fusion, f32[1280]{0:T(1024)S(1)} %get-tuple-element.144, ...), channel_id=1, replica_groups=mesh['rep'=8,'fsdp'=2,'ctx'=2] {'rep','fsdp','ctx'}, use_global_device_ids=true, to_apply=%region_24.25 | all-reduce | flops 5200 | bytes 41600 | tf_op jit(solution)/shard_map/psum | solution.py:240
  965.5 114.8 %all-reduce.4.cloned.1.call-done = (bf16[320,1280]{1,0:T(8,128)(2,1)}, bf16[320,1280]{1,0:T(8,128)(2,1)}, bf16[320,1280]{1,0:T(8,128)(2,1)}, bf16[320,1280]{1,0:...) async-done(((bf16[320,1280]{1,0:T(8,128)(2,1)}, bf16[320,1280]{1,0:T(8,128)(2,1)}, bf16[320,1280]{1,0:T(8,128)(2,1)}, bf16[320,1280]{1,0:T(8,128)(2,1)}, ...) | async-done | bytes 4915216 | tf_op jit(solution)/shard_map/psum | solution.py:233
  (254 shorter events, 394.0 us)
Async XLA Ops:
  7.2 19.4 %copy-start.26 = (f32[1280]{0:T(1024)S(1)}, f32[1280]{0:T(1024)}, u32[]{:S(2)}) copy-start(f32[1280]{0:T(1024)} %param.28) | copy-start | bytes 15364
  7.2 91.6 %all-gather.9.cloned.1.call-start = ((), (), s32[]{:S(2)}) async-start(), calls=%async_computation.8 | async-start | bytes 4096000 | tf_op jit(solution)/shard_map/all_gather | solution.py:68
  7.9 107.6 %all-gather.13.cloned.1.call-start = ((), (), s32[]{:S(2)}) async-start(), calls=%async_computation.10 | async-start | bytes 4096000 | tf_op jit(solution)/shard_map/all_gather | solution.py:66
  8.7 121.4 %all-gather.15.cloned.1.call-start = ((), (), s32[]{:S(2)}) async-start(), calls=%async_computation.11 | async-start | bytes 7864320 | tf_op jit(solution)/shard_map/all_gather | solution.py:92
  8.7 14.5 %collective-permute-start = (bf16[320,1280]{1,0:T(8,128)(2,1)}, bf16[320,1280]{1,0:T(8,128)(2,1)}, u32[]{:S(2)}, u32[]{:S(2)}) collective-permute-start(bf16[320,1280]{1,0:T(8,128)(2,1)} %param.21), channel_id=1, source_target_pairs={{0,3},{1,0},{2,1},{3,2},{4,7},{5,4},{6,5},{7,6},{8,11},{9,8},{10,9... | collective-permute-start | bytes 2457608 | tf_op jit(solution)/shard_map/ppermute | solution.py:17
  25.9 59.1 %collective-permute-start.1 = (bf16[640,1280]{1,0:T(8,128)(2,1)}, bf16[640,1280]{1,0:T(8,128)(2,1)}, u32[]{:S(2)}, u32[]{:S(2)}) collective-permute-start(bf16[640,1280]{1,0:T(8,128)(2,1)} %pad_maximum_fusion), channel_id=1, source_target_pairs={{0,2},{1,3},{2,0},{3,1},{4,6},{5,7},{6,4},{7,5},{8,10},{9,11},{10,... | collective-permute-start | bytes 4915208 | tf_op jit(solution)/shard_map/ppermute | solution.py:17
  26.5 60.0 %copy-start.28 = (f32[1,4,2,128]{3,1,2,0:T(4,128)}, f32[1,4,2,128]{3,1,2,0:T(4,128)S(1)}, u32[]{:S(2)}) copy-start(f32[1,4,2,128]{3,1,2,0:T(4,128)S(1)} %copy.64) | copy-start | bytes 12292
  27.3 62.1 %copy-start.18 = (bf16[1024,1280]{1,0:T(8,128)(2,1)}, bf16[1024,1280]{1,0:T(8,128)(2,1)S(1)}, u32[]{:S(2)}) copy-start(bf16[1024,1280]{1,0:T(8,128)(2,1)S(1)} %fusion.39) | copy-start | bytes 7864324
  98.7 36.1 %all-gather.11.cloned.1.call-start = ((), (), s32[]{:S(2)}) async-start(), calls=%async_computation.9 | async-start | bytes 7864320 | tf_op jit(solution)/shard_map/all_gather | solution.py:93
  111.2 136.0 %all-gather.17.cloned.1.call-start = ((), (), s32[]{:S(2)}) async-start(), calls=%async_computation.12 | async-start | bytes 4096000 | tf_op jit(solution)/shard_map/all_gather | solution.py:69
  111.8 145.1 %all-gather.19.cloned.1.call-start = ((), (), s32[]{:S(2)}) async-start(), calls=%async_computation.13 | async-start | bytes 4096000 | tf_op jit(solution)/shard_map/all_gather | solution.py:70
  112.3 153.9 %all-gather.21.cloned.1.call-start = ((), (), s32[]{:S(2)}) async-start(), calls=%async_computation.14 | async-start | bytes 4096000 | tf_op jit(solution)/shard_map/all_gather | solution.py:71
  113.1 513.2 %reduce-scatter.11.cloned.1.call-start = ((), (), s32[]{:S(2)}) async-start(), calls=%async_computation.17 | async-start | bytes 15728640 | tf_op jit(solution)/shard_map/reduce_scatter | solution.py:187
  256.9 24.0 %copy-start.30 = (f32[1024]{0:T(1024)}, f32[1024]{0:T(1024)S(1)}, u32[]{:S(2)}) copy-start(f32[1024]{0:T(1024)S(1)} %get-tuple-element.206) | copy-start | bytes 12292
  579.7 56.0 %reduce-scatter.9.cloned.1.call-start = ((), (), s32[]{:S(2)}) async-start(), calls=%async_computation.15 | async-start | bytes 15728640 | tf_op jit(solution)/shard_map/reduce_scatter | solution.py:186
  580.5 82.7 %reduce-scatter.23.cloned.1.call-start = ((), (), s32[]{:S(2)}) async-start(), calls=%async_computation.23 | async-start | bytes 4096000 | tf_op jit(solution)/shard_map/reduce_scatter | solution.py:228
  590.6 114.0 %reduce-scatter.21.cloned.1.call-start = ((), (), s32[]{:S(2)}) async-start(), calls=%async_computation.22 | async-start | bytes 4096000 | tf_op jit(solution)/shard_map/reduce_scatter | solution.py:225
  602.1 143.6 %reduce-scatter.19.cloned.1.call-start = ((), (), s32[]{:S(2)}) async-start(), calls=%async_computation.21 | async-start | bytes 4096000 | tf_op jit(solution)/shard_map/reduce_scatter | solution.py:222
  609.6 177.4 %reduce-scatter.13.cloned.1.call-start = ((), (), s32[]{:S(2)}) async-start(), calls=%async_computation.18 | async-start | bytes 4096000 | tf_op jit(solution)/shard_map/reduce_scatter | solution.py:213
  626.2 202.0 %reduce-scatter.17.cloned.1.call-start = ((), (), s32[]{:S(2)}) async-start(), calls=%async_computation.20 | async-start | bytes 4096000 | tf_op jit(solution)/shard_map/reduce_scatter | solution.py:219
  635.7 233.7 %reduce-scatter.15.cloned.1.call-start = ((), (), s32[]{:S(2)}) async-start(), calls=%async_computation.19 | async-start | bytes 4096000 | tf_op jit(solution)/shard_map/reduce_scatter | solution.py:216
  645.0 255.0 %all-gather.23.cloned.1.call-start = ((), (), s32[]{:S(2)}) async-start(), calls=%async_computation.16 | async-start | bytes 4096000 | tf_op jit(solution)/shard_map/all_gather | solution.py:125
  645.6 434.7 %all-reduce.4.cloned.1.call-start = ((), (), s32[]{:S(2)}) async-start(), calls=%async_computation.24 | async-start | bytes 9830400 | tf_op jit(solution)/shard_map/psum | solution.py:233
  647.2 222.1 %copy-start.40 = (f32[1280]{0:T(1024)S(1)}, f32[1280]{0:T(1024)}, u32[]{:S(2)}) copy-start(f32[1280]{0:T(1024)} %param.27) | copy-start | bytes 15364
  (49 other events, 364.1 us)
Sparse Core Ops, SparseCore 0:
  9.6 42.6 all-gather.8
  53.8 40.4 all-gather.12
  98.8 17.5 all-gather.14
  118.4 16.3 all-gather.10
  136.2 30.4 all-gather.16
  168.1 29.2 all-gather.18
  199.0 29.2 all-gather.20
  579.9 19.2 reduce-scatter.10
  601.5 19.2 reduce-scatter.8
  623.2 39.9 reduce-scatter.22
  665.8 38.6 reduce-scatter.20
  707.0 38.6 reduce-scatter.18
  748.3 38.6 reduce-scatter.12
  789.4 38.6 reduce-scatter.16
  830.6 38.6 reduce-scatter.14
  870.7 29.2 all-gather.22
  904.2 176.0 all-reduce.3
